TPU v7x, 32 devices: a whole 2x2x4 slice. The times are simulated.
32 devices in a mesh: vocab: 8 (over z, y), section: 4 (over x, core).
Axes of the slice: x: 2, y: 2, z: 4, core: 2. Of those that a mesh axis runs over, the one named last changes fastest.
Arguments:
- hidden: bfloat16 [512, 8192], P('section', 'vocab'), may hold values from -2 to 2
- targets: int32 [512], replicated, may hold values from 0 to 12287
- out_weight: bfloat16 [12288, 8192], P(('vocab', 'section')), may hold values from -2 to 2
Outputs:
- token_loss: float32 [512], replicated
- weight_grad: bfloat16 [12288, 8192], P(('vocab', 'section'))
- sent_grad: bfloat16 [512, 8192], P('section', 'vocab')
All inputs are finite; a program needn't handle non-finite values.
Results may differ from a plain program's by a relative error of at most 0.0033.
Values may be sent and summed in bfloat16 or wider, within the bound.
No kernel may reach another device: no remote copies, remote signals or barrier semaphores. Data moves between devices by JAX's collectives and lax.ppermute only.
A program may use at most 128 MiB of HBM per device.

v0:
```python
import jax
import jax.numpy as jnp
from jax import lax
from jax.sharding import PartitionSpec as P


def shifted(value, axis, steps):
    count = lax.axis_size(axis)
    pairs = [(source, (source + steps) % count) for source in range(count)]
    return lax.ppermute(value, axis, pairs)


def on_device(hidden, targets, out_weight):
    columns = lax.all_gather(hidden, "vocab", axis=1, tiled=True)
    whole = lax.all_gather(columns, "section", axis=0, tiled=True)
    rows = out_weight.shape[0]
    offset = lax.axis_index(("vocab", "section")) * rows
    logits = jnp.einsum("td,vd->tv", whole, out_weight, preferred_element_type=jnp.float32)
    picked = targets[:, None] - offset == jnp.arange(rows, dtype=jnp.int32)[None, :]
    local_hit = jnp.sum(jnp.where(picked, logits, jnp.float32(0.0)), axis=1)
    local_top = jnp.max(logits, axis=1)
    top = lax.pmax(local_top, ("vocab", "section"))
    local_sum = jnp.sum(jnp.exp(logits - top[:, None]), axis=1)
    total, target_logit = lax.psum((local_sum, local_hit), ("vocab", "section"))
    token_loss = top + jnp.log(total) - target_logit
    probs = jnp.exp(logits - top[:, None]) / total[:, None]
    dlogits = (probs - picked.astype(jnp.float32)).astype(jnp.bfloat16)
    weight_grad = jnp.einsum(
        "tv,td->vd", dlogits, whole, preferred_element_type=jnp.float32
    ).astype(jnp.bfloat16)
    token_block = lax.psum_scatter(
        jnp.dot(dlogits, out_weight, preferred_element_type=jnp.float32),
        "section",
        scatter_dimension=0,
        tiled=True,
    )
    owned = lax.psum_scatter(token_block, "vocab", scatter_dimension=1, tiled=True)
    sent_grad = shifted(owned.astype(jnp.bfloat16), "section", -1)
    return (token_loss, weight_grad, sent_grad)


def solution(mesh):
    in_specs = (P("section", "vocab"), P(), P(("vocab", "section"), None))
    out_specs = (P(), P(("vocab", "section"), None), P("section", "vocab"))
    return jax.shard_map(
        on_device, mesh=mesh, in_specs=in_specs, out_specs=out_specs, check_vma=False
    )
```

profile of v0, /device:TPU:0, one launch (start us, length us, event | category | flops | bytes accessed | tf_op | source)
XLA Modules:
  0.0 455.0 jit_solution(5437715130508668706)
XLA Ops:
  7.2 0.0 all-gather.3.cloned.1.call-start
  7.2 0.7 all-gather.3.cloned.1.call-update
  7.9 0.0 all-gather.5.cloned.1.call-start
  7.9 54.0 %all-gather.3.cloned.1.call-done = bf16[128,8192]{1,0:T(8,128)(2,1)} async-done(((bf16[128,1024]{1,0:T(8,128)(2,1)}), bf16[128,8192]{1,0:T(8,128)(2,1)}) %all-gather.3.cloned.1.call-update) | async-done | bytes 2097168 | tf_op jit(solution)/shard_map/all_gather | solution.py:14
  62.0 0.0 all-gather.5.cloned.1.call-update
  62.0 0.0 reduce-scatter.3.cloned.1.call-start
  62.1 0.7 broadcast_subtract_fusion
  62.7 57.6 %all-gather.5.cloned.1.call-done = bf16[512,8192]{1,0:T(8,128)(2,1)} async-done(((bf16[128,8192]{1,0:T(8,128)(2,1)}), bf16[512,8192]{1,0:T(8,128)(2,1)}) %all-gather.5.cloned.1.call-update) | async-done | bytes 8388624 | tf_op jit(solution)/shard_map/all_gather | solution.py:15
  120.4 7.8 %fusion.2 = (f32[512]{0:T(512)S(1)}, f32[512,384]{0,1:T(8,128)S(1)}) fusion(bf16[512,8192]{1,0:T(8,128)(2,1)} %all-gather.5.cloned.1.call-done, bf16[384,8192]{1,0:T(8,128)(2,1)} %param.5), kind=kOutput, calls=%fused_computation.9 | convolution fusion | flops 3221421568 | bytes 15468544 | tf_op jit(solution)/shard_map/td,vd->tv/dot_general | solution.py:18
  128.2 39.3 %pmax.7 = f32[512]{0:T(512)S(1)} all-reduce(f32[512]{0:T(512)S(1)} %get-tuple-element.7), channel_id=1, replica_groups=mesh['vocab'=8,'section'=4] {'vocab','section'}, use_global_device_ids=true, to_apply=%region_1.2 | all-reduce | flops 512 | bytes 4096 | tf_op jit(solution)/shard_map/pmax | solution.py:22
  167.5 0.2 fusion
  167.7 40.9 %all-reduce = (f32[512]{0:T(512)S(1)}, f32[512]{0:T(512)S(1)}) all-reduce(f32[512]{0:T(512)S(1)} %get-tuple-element.4, f32[512]{0:T(512)S(1)} %get-tuple-element.3), channel_id=1, replica_groups=mesh['vocab'=8,'section'=4] {'vocab','section'}, use_global_device_ids=true, to_apply=%region_5.6 | all-reduce | flops 1024 | bytes 8192 | tf_op jit(solution)/shard_map/psum | solution.py:24
  208.7 10.9 %fusion.1 = f32[512,8192]{1,0:T(8,128)} fusion(bf16[384,8192]{1,0:T(8,128)(2,1)} %param.5, f32[512,384]{0,1:T(8,128)S(1)} %get-tuple-element.8, f32[512]{0:T(512)S(1)} %get-tuple-element.6, s32[512]{0:T(512)S(1)} %broadcast_subtract_fusion, f32[512]{0:T(512)S(1)} %pmax.7), kind=kOutput, calls=%fused_computation.8 | convolution fusion | flops 3222405120 | bytes 23861248 | tf_op jit(solution)/shard_map/dot_general | solution.py:32
  219.6 0.0 reduce-scatter.3.cloned.1.call-update
  219.6 0.0 reduce-scatter.5.cloned.1.call-start
  219.7 125.0 %reduce-scatter.3.cloned.1.call-done = f32[128,8192]{1,0:T(8,128)} async-done(((f32[512,8192]{1,0:T(8,128)}), f32[128,8192]{1,0:T(8,128)}) %reduce-scatter.3.cloned.1.call-update) | async-done | bytes 4194320 | tf_op jit(solution)/shard_map/reduce_scatter | solution.py:31
  344.6 0.0 reduce-scatter.5.cloned.1.call-update
  344.6 92.2 %reduce-scatter.5.cloned.1.call-done = f32[128,1024]{1,0:T(8,128)} async-done(((f32[128,8192]{1,0:T(8,128)}), f32[128,1024]{1,0:T(8,128)}) %reduce-scatter.5.cloned.1.call-update) | async-done | bytes 524304 | tf_op jit(solution)/shard_map/reduce_scatter | solution.py:37
  436.8 1.1 convert_element_type.15
  437.9 0.6 collective-permute-start
  438.5 8.7 %convolution_convert_fusion = bf16[384,8192]{1,0:T(8,128)(2,1)} fusion(bf16[512,8192]{1,0:T(8,128)(2,1)} %all-gather.5.cloned.1.call-done, f32[512,384]{0,1:T(8,128)S(1)} %get-tuple-element.8, f32[512]{0:T(512)S(1)} %get-tuple-element.6, s32[512]{0:T(512)S(1)} %broadcast_subtract_fusion, f32[512]{0:T(512)S(1)} %pmax.7), kind=kOutput, calls=%fused_computation | convolution fusion | flops 3225550848 | bytes 15472640 | tf_op jit(solution)/shard_map/tv,td->vd/dot_general | solution.py:28
  447.2 0.6 add_subtract_fusion
  447.8 0.0 collective-permute-done
  447.8 0.7 copy.7
Async XLA Ops:
  7.2 54.8 %all-gather.3.cloned.1.call-start = ((), (), s32[]{:S(2)}) async-start(), calls=%async_computation.2 | async-start | bytes 2359296 | tf_op jit(solution)/shard_map/all_gather | solution.py:14
  7.9 112.5 %all-gather.5.cloned.1.call-start = ((), (), s32[]{:S(2)}) async-start(), calls=%async_computation.3 | async-start | bytes 10485760 | tf_op jit(solution)/shard_map/all_gather | solution.py:15
  62.0 282.6 %reduce-scatter.3.cloned.1.call-start = ((), (), s32[]{:S(2)}) async-start(), calls=%async_computation.4 | async-start | bytes 20971520 | tf_op jit(solution)/shard_map/reduce_scatter | solution.py:31
  219.6 217.2 %reduce-scatter.5.cloned.1.call-start = ((), (), s32[]{:S(2)}) async-start(), calls=%async_computation.5 | async-start | bytes 4718592 | tf_op jit(solution)/shard_map/reduce_scatter | solution.py:37
  437.9 9.9 %collective-permute-start = (bf16[128,1024]{1,0:T(8,128)(2,1)S(1)}, bf16[128,1024]{1,0:T(8,128)(2,1)S(1)}, u32[]{:S(2)}, u32[]{:S(2)}) collective-permute-start(bf16[128,1024]{1,0:T(8,128)(2,1)S(1)} %convert_element_type.15), channel_id=1, source_target_pairs={{0,3},{1,0},{2,1},{3,2},{4,7},{5,4},{6,5},{7,6},{8,11},{9,8},{10,9... | collective-permute-start | bytes 786440 | tf_op jit(solution)/shard_map/ppermute | solution.py:10
Sparse Core Ops, SparseCore 0:
  10.2 51.7 all-gather.2
  63.5 56.7 all-gather.4
  219.7 124.8 reduce-scatter.2
  348.1 88.6 reduce-scatter.4
where the time goes:
time: 456 us; the launch traced here: 455 us
  waiting for transfers between devices  330 us (72%)
  blocking collectives  80.2 us (18%)
  matrix products  27.5 us (6%)
  between operations  13.8 us (3%)
    reduce_scatter x1, waiting for transfers between devices, on_device(): lax.psum_scatter(jnp.dot(dlogits, out_weight, preferred_element_type=jnp....  125 us
    reduce_scatter x1, waiting for transfers between devices, on_device(): lax.psum_scatter(token_block, 'vocab', scatter_dimension=1, tiled=True)  92.2 us
    all_gather x1, waiting for transfers between devices, on_device(): whole = lax.all_gather(columns, 'section', axis=0, tiled=True)  57.6 us
    all_gather x1, waiting for transfers between devices, on_device(): columns = lax.all_gather(hidden, 'vocab', axis=1, tiled=True)  54 us
    psum x1, blocking collectives, on_device(): total, target_logit = lax.psum((local_sum, local_hit), ('vocab', 'section'))  40.9 us
    pmax x1, blocking collectives, on_device(): top = lax.pmax(local_top, ('vocab', 'section'))  39.3 us
    dot_general x1, matrix products, on_device(): jnp.dot(dlogits, out_weight, preferred_element_type=jnp.float32)  10.9 us
  transfers between devices with their start and end apart: 5, of which 4 were waited for; matrix products, arithmetic and copies ran while one was open for 2% of the time, Pallas kernels for 0%

commit v1 on v0

--- a/solution.py
+++ b/solution.py
@@ -21,7 +21,7 @@
     local_top = jnp.max(logits, axis=1)
     top = lax.pmax(local_top, ("vocab", "section"))
     local_sum = jnp.sum(jnp.exp(logits - top[:, None]), axis=1)
-    total, target_logit = lax.psum((local_sum, local_hit), ("vocab", "section"))
+    total, target_logit = jax.lax.psum(jax.lax.psum((local_sum, local_hit), "vocab"), "section")
     token_loss = top + jnp.log(total) - target_logit
     probs = jnp.exp(logits - top[:, None]) / total[:, None]
     dlogits = (probs - picked.astype(jnp.float32)).astype(jnp.bfloat16)

time: 456 us -> 439 us (0.963)
  blocking collectives: 80.2 us -> 66 us
    psum x1 -> x2, blocking collectives: 40.9 us -> 26.7 us  [the longest x1 21.1 us: on_device(): jax.lax.psum((local_sum, local_hit), 'vocab')]
where the time goes in v1:
time: 439 us
  waiting for transfers between devices  327 us (74%)
  blocking collectives  66 us (15%)
  matrix products  27.5 us (6%)
  between operations  13.8 us (3%)
    reduce_scatter x1, waiting for transfers between devices, on_device(): lax.psum_scatter(jnp.dot(dlogits, out_weight, preferred_element_type=jnp....  123 us
    reduce_scatter x1, waiting for transfers between devices, on_device(): lax.psum_scatter(token_block, 'vocab', scatter_dimension=1, tiled=True)  92.2 us
    all_gather x1, waiting for transfers between devices, on_device(): whole = lax.all_gather(columns, 'section', axis=0, tiled=True)  57.6 us
    all_gather x1, waiting for transfers between devices, on_device(): columns = lax.all_gather(hidden, 'vocab', axis=1, tiled=True)  54 us
    pmax x1, blocking collectives, on_device(): top = lax.pmax(local_top, ('vocab', 'section'))  39.3 us
    psum x1, blocking collectives, on_device(): jax.lax.psum((local_sum, local_hit), 'vocab')  21.1 us
    dot_general x1, matrix products, on_device(): jnp.dot(dlogits, out_weight, preferred_element_type=jnp.float32)  10.9 us
  transfers between devices with their start and end apart: 5, of which 4 were waited for; matrix products, arithmetic and copies ran while one was open for 2% of the time, Pallas kernels for 0%

profile of v1, /device:TPU:0, one launch (start us, length us, event | category | flops | bytes accessed | tf_op | source)
XLA Modules:
  0.0 438.5 jit_solution(4416608637661241769)
XLA Ops:
  7.2 0.0 all-gather.3.cloned.1.call-start
  7.2 0.7 all-gather.3.cloned.1.call-update
  7.9 0.0 all-gather.5.cloned.1.call-start
  7.9 54.0 %all-gather.3.cloned.1.call-done = bf16[128,8192]{1,0:T(8,128)(2,1)} async-done(((bf16[128,1024]{1,0:T(8,128)(2,1)}), bf16[128,8192]{1,0:T(8,128)(2,1)}) %all-gather.3.cloned.1.call-update) | async-done | bytes 2097168 | tf_op jit(solution)/shard_map/all_gather | solution.py:14
  62.0 0.0 all-gather.5.cloned.1.call-update
  62.0 0.0 reduce-scatter.3.cloned.1.call-start
  62.1 0.7 broadcast_subtract_fusion
  62.7 57.6 %all-gather.5.cloned.1.call-done = bf16[512,8192]{1,0:T(8,128)(2,1)} async-done(((bf16[128,8192]{1,0:T(8,128)(2,1)}), bf16[512,8192]{1,0:T(8,128)(2,1)}) %all-gather.5.cloned.1.call-update) | async-done | bytes 8388624 | tf_op jit(solution)/shard_map/all_gather | solution.py:15
  120.4 7.8 %fusion.2 = (f32[512]{0:T(512)S(1)}, f32[512,384]{0,1:T(8,128)S(1)}) fusion(bf16[512,8192]{1,0:T(8,128)(2,1)} %all-gather.5.cloned.1.call-done, bf16[384,8192]{1,0:T(8,128)(2,1)} %param.5), kind=kOutput, calls=%fused_computation.9 | convolution fusion | flops 3221421568 | bytes 15468544 | tf_op jit(solution)/shard_map/td,vd->tv/dot_general | solution.py:18
  128.2 39.3 %pmax.7 = f32[512]{0:T(512)S(1)} all-reduce(f32[512]{0:T(512)S(1)} %get-tuple-element.9), channel_id=1, replica_groups=mesh['vocab'=8,'section'=4] {'vocab','section'}, use_global_device_ids=true, to_apply=%region_1.2 | all-reduce | flops 512 | bytes 4096 | tf_op jit(solution)/shard_map/pmax | solution.py:22
  167.5 0.2 fusion
  167.8 21.1 %all-reduce = (f32[512]{0:T(512)S(1)}, f32[512]{0:T(512)S(1)}) all-reduce(f32[512]{0:T(512)S(1)} %get-tuple-element.4, f32[512]{0:T(512)S(1)} %get-tuple-element.3), channel_id=1, replica_groups=mesh['vocab'=8,'section'=4] {'vocab'}, use_global_device_ids=true, to_apply=%region_6.7 | all-reduce | flops 1024 | bytes 8192 | tf_op jit(solution)/shard_map/psum | solution.py:24
  188.8 5.6 %all-reduce.1 = (f32[512]{0:T(512)S(1)}, f32[512]{0:T(512)S(1)}) all-reduce(f32[512]{0:T(512)S(1)} %get-tuple-element.5, f32[512]{0:T(512)S(1)} %get-tuple-element.6), channel_id=1, replica_groups=mesh['vocab'=8,'section'=4] {'section'}, use_global_device_ids=true, to_apply=%region_7.8 | all-reduce | flops 1024 | bytes 8192 | tf_op jit(solution)/shard_map/psum | solution.py:24
  194.5 10.9 %fusion.1 = f32[512,8192]{1,0:T(8,128)} fusion(bf16[384,8192]{1,0:T(8,128)(2,1)} %param.5, f32[512,384]{0,1:T(8,128)S(1)} %get-tuple-element.10, f32[512]{0:T(512)S(1)} %get-tuple-element.8, s32[512]{0:T(512)S(1)} %broadcast_subtract_fusion, f32[512]{0:T(512)S(1)} %pmax.7), kind=kOutput, calls=%fused_computation.8 | convolution fusion | flops 3222405120 | bytes 23861248 | tf_op jit(solution)/shard_map/dot_general | solution.py:32
  205.4 0.0 reduce-scatter.3.cloned.1.call-update
  205.4 0.0 reduce-scatter.5.cloned.1.call-start
  205.5 122.7 %reduce-scatter.3.cloned.1.call-done = f32[128,8192]{1,0:T(8,128)} async-done(((f32[512,8192]{1,0:T(8,128)}), f32[128,8192]{1,0:T(8,128)}) %reduce-scatter.3.cloned.1.call-update) | async-done | bytes 4194320 | tf_op jit(solution)/shard_map/reduce_scatter | solution.py:31
  328.1 0.0 reduce-scatter.5.cloned.1.call-update
  328.1 92.2 %reduce-scatter.5.cloned.1.call-done = f32[128,1024]{1,0:T(8,128)} async-done(((f32[128,8192]{1,0:T(8,128)}), f32[128,1024]{1,0:T(8,128)}) %reduce-scatter.5.cloned.1.call-update) | async-done | bytes 524304 | tf_op jit(solution)/shard_map/reduce_scatter | solution.py:37
  420.3 1.1 convert_element_type.15
  421.4 0.6 collective-permute-start
  422.0 8.7 %convolution_convert_fusion = bf16[384,8192]{1,0:T(8,128)(2,1)} fusion(bf16[512,8192]{1,0:T(8,128)(2,1)} %all-gather.5.cloned.1.call-done, f32[512,384]{0,1:T(8,128)S(1)} %get-tuple-element.10, f32[512]{0:T(512)S(1)} %get-tuple-element.8, s32[512]{0:T(512)S(1)} %broadcast_subtract_fusion, f32[512]{0:T(512)S(1)} %pmax.7), kind=kOutput, calls=%fused_computation | convolution fusion | flops 3225550848 | bytes 15472640 | tf_op jit(solution)/shard_map/tv,td->vd/dot_general | solution.py:28
  430.7 0.6 add_subtract_fusion
  431.3 0.0 collective-permute-done
  431.3 0.7 copy.7
Async XLA Ops:
  7.2 54.8 %all-gather.3.cloned.1.call-start = ((), (), s32[]{:S(2)}) async-start(), calls=%async_computation.2 | async-start | bytes 2359296 | tf_op jit(solution)/shard_map/all_gather | solution.py:14
  7.9 112.5 %all-gather.5.cloned.1.call-start = ((), (), s32[]{:S(2)}) async-start(), calls=%async_computation.3 | async-start | bytes 10485760 | tf_op jit(solution)/shard_map/all_gather | solution.py:15
  62.0 266.1 %reduce-scatter.3.cloned.1.call-start = ((), (), s32[]{:S(2)}) async-start(), calls=%async_computation.4 | async-start | bytes 20971520 | tf_op jit(solution)/shard_map/reduce_scatter | solution.py:31
  205.4 214.9 %reduce-scatter.5.cloned.1.call-start = ((), (), s32[]{:S(2)}) async-start(), calls=%async_computation.5 | async-start | bytes 4718592 | tf_op jit(solution)/shard_map/reduce_scatter | solution.py:37
  421.4 9.9 %collective-permute-start = (bf16[128,1024]{1,0:T(8,128)(2,1)S(1)}, bf16[128,1024]{1,0:T(8,128)(2,1)S(1)}, u32[]{:S(2)}, u32[]{:S(2)}) collective-permute-start(bf16[128,1024]{1,0:T(8,128)(2,1)S(1)} %convert_element_type.15), channel_id=1, source_target_pairs={{0,3},{1,0},{2,1},{3,2},{4,7},{5,4},{6,5},{7,6},{8,11},{9,8},{10,9... | collective-permute-start | bytes 786440 | tf_op jit(solution)/shard_map/ppermute | solution.py:10
Sparse Core Ops, SparseCore 0:
  10.2 51.7 all-gather.2
  63.5 56.7 all-gather.4
  205.5 122.5 reduce-scatter.2
  331.6 88.6 reduce-scatter.4
